TPU v7x, 32 devices: a whole 2x2x4 slice. The times are simulated.
32 devices in a mesh: depth: 4 (over x, core), rows: 8 (over z, y).
Axes of the slice: x: 2, y: 2, z: 4, core: 2. Of those that a mesh axis runs over, the one named last changes fastest.
Arguments:
- volume: bfloat16 [4, 64, 256, 4096], P(None, 'depth', 'rows')
- shear_rows: int32 [64], P('depth'), may hold values from -8 to 8, as said below
- shear_cols: int32 [64], P('depth'), may hold values from -8 to 8, as said below
- warp_cols: int32 [256], replicated, may hold values from -8 to 8, as said below
- warp_rows: int32 [4096], P('depth'), may hold values from -8 to 8, as said below
Outputs:
- final_image: float32 [4, 256, 4096], P(None, 'rows', 'depth')
Inputs may be any that keep to these rules, and one draw needn't show every extreme that they name: `shear_rows`: both -8 and 8 occur. `shear_cols`: both -8 and 8 occur. `warp_cols`: both -8 and 8 occur. `warp_rows`: both -8 and 8 occur.
All inputs are finite; a program needn't handle non-finite values.
Results may differ from a plain program's by a relative error of at most 0.0017.
Values may be sent and summed in bfloat16 or wider, within the bound.
A program may use at most 192 MiB of HBM per device.

v0:
```python
import functools

import jax
import jax.numpy as jnp
from jax import lax
from jax.experimental import pallas as pl
from jax.experimental.pallas import tpu as pltpu
from jax.sharding import PartitionSpec as P

SHIFT = 8
RIM = SHIFT + 1
GROUP = 8
EDGE = 16
LANES = 128
LEAD = 16
CHUNK = 512
BF = jnp.bfloat16
F32 = jnp.float32
MESH = pl.DeviceIdType.MESH


def weight_of(offset):
    return jnp.where(offset == 0, 0.5, jnp.where(jnp.abs(offset) == 1, 0.25, 0.0)).astype(F32)


def iota(shape, dim):
    return lax.broadcasted_iota(jnp.int32, shape, dim)


def groups_of(s, ou, od, total):
    gu = jnp.minimum(ou // GROUP, total - jnp.where(s > 0, 2, 1))
    gd = jnp.minimum(od // GROUP, total - jnp.where(s < 0, 2, 1))
    g0 = jnp.where(s >= 0, gu, total + gd)
    g1 = jnp.where(s > 0, gu + 1, total + gd + jnp.where(s < 0, 1, 0))
    return gu, gd, g0, g1


def slab_kernel(
    sizes, row_s, col_s, off_up, off_dn, at_up_ref, at_dn_ref, warp_ref, vol_hbm,
    mid_ref, low_ref, high_ref,
    vol, send_up, send_dn, recv_up, recv_dn, work, w_row, w_col, band, acc, outb, parts, wide_ref,
    load_sem, s_up, r_up, s_dn, r_dn, s_part, r_part,
):
    depth, n_rows = sizes
    chunks, channels, slab, rows, _ = vol.shape
    groups = send_up.shape[1]
    high = groups * GROUP
    cols = chunks * CHUNK
    tile = cols // depth
    per = CHUNK // LANES
    per_tile = tile // LANES
    pieces = tile // CHUNK
    flat = channels * rows
    me = lax.axis_index("depth")
    row = lax.axis_index("rows")
    has_up = row < n_rows - 1
    has_dn = row > 0
    above = jnp.maximum(row - 1, 0)
    below = jnp.minimum(row + 1, n_rows - 1)

    def load(i):
        return pltpu.make_async_copy(
            vol_hbm.at[:, :, :, pl.ds(pl.multiple_of(i * CHUNK, CHUNK), CHUNK)], vol.at[i], load_sem.at[i]
        )

    for i in range(chunks):
        load(i).start()

    barrier = pltpu.get_barrier_semaphore()
    for r in (lax.rem(row + 1, n_rows), lax.rem(row + n_rows - 1, n_rows)):
        pl.semaphore_signal(barrier, inc=1, device_id=(me, r), device_id_type=MESH)
    for m in range(1, depth):
        pl.semaphore_signal(barrier, inc=1, device_id=(lax.rem(me + m, depth), row), device_id_type=MESH)
    pl.semaphore_wait(barrier, depth + 1)

    def up_copy(i):
        return pltpu.make_async_remote_copy(
            send_up.at[i], recv_up.at[i], s_up.at[i], r_up.at[i], device_id=(me, above), device_id_type=MESH
        )

    def dn_copy(i):
        return pltpu.make_async_remote_copy(
            send_dn.at[i], recv_dn.at[i], s_dn.at[i], r_dn.at[i], device_id=(me, below), device_id_type=MESH
        )

    def send(i):
        @pl.when(has_dn)
        def _():
            up_copy(i).start()

        @pl.when(has_up)
        def _():
            dn_copy(i).start()

    @pl.loop(0, chunks)
    def _(i):
        load(i).wait()
        for at_ref, out, first in ((at_up_ref, send_up, 0), (at_dn_ref, send_dn, rows - EDGE)):
            pick = (iota((high, slab * EDGE), 0) == at_ref[...]).astype(F32).astype(BF)
            got = []
            for c in range(channels):
                source = vol[i, c, :, first : first + EDGE, :].reshape(slab * EDGE, CHUNK)
                got.append(jnp.dot(pick, source, preferred_element_type=F32))
            got = [g * got[-1] for g in got[:-1]] + [got[-1]]
            for g in range(groups):
                piece = [v[g * GROUP : (g + 1) * GROUP] for v in got]
                out[i, g] = jnp.concatenate(piece, 0).astype(BF)

        @pl.when(i > 0)
        def _():
            send(i - 1)

    send(chunks - 1)

    work[...] = jnp.zeros_like(work)
    band[...] = jnp.zeros_like(band)

    @pl.loop(0, slab)
    def _(k):
        s = row_s[k]
        ou = off_up[k]
        od = off_dn[k]
        gu, gd, _, _ = groups_of(s, ou, od, groups)
        count = jnp.maximum(0, 1 - s)
        row_up = rows + gu * GROUP - ou
        row_dn = gd * GROUP - od - count
        m = iota((flat, flat), 0)
        j = iota((flat, flat), 1)
        same = (m // rows) == (j // rows)
        w_row[k, :, :flat] = jnp.where(same, weight_of((j % rows) - (m % rows) - s), 0.0).astype(BF)
        wide = 2 * channels * GROUP
        m = iota((flat, wide), 0)
        j = iota((flat, wide), 1)
        second = j >= channels * GROUP
        q = j % GROUP
        same = (m // rows) == ((j // GROUP) % channels)
        first_row = jnp.where(s >= 0, row_up, row_dn)
        second_row = jnp.where(s > 0, row_up + GROUP, row_dn + jnp.where(s < 0, GROUP, 0))
        r = q + jnp.where(second, second_row, first_row)
        room = jnp.where(second, jnp.where(s > 0, r - rows, -1 - r), jnp.where(s >= 0, r - rows, -1 - r))
        kept = same & (room >= 0)
        w_row[k, :, flat : flat + wide] = jnp.where(kept, weight_of(r - (m % rows) - s), 0.0).astype(BF)
        shape = (2 * LANES, LANES)
        offset = iota(shape, 0) - iota(shape, 1) - (LANES - LEAD) - col_s[k]
        w_col[k] = weight_of(offset).astype(BF)

    def part_copy(i, w, count, owner, at, piece):
        return pltpu.make_async_remote_copy(
            outb.at[pl.ds(i * per + w, count)],
            parts.at[me, pl.ds(at, count)],
            s_part.at[i, piece],
            r_part.at[me, pieces if piece else lax.rem(i, pieces)],
            device_id=(owner, row),
            device_id_type=MESH,
        )

    def deliver(i, act, keep):
        owner = i // pieces
        at = lax.rem(i, pieces) * per

        @pl.when(owner != me)
        def _():
            act(part_copy(i, 0, per, owner, at, 0))

        if keep:
            @pl.when(owner == me)
            def _():
                parts[me, pl.ds(at, per)] = outb[pl.ds(i * per, per)]

        margin = (lax.rem(i, pieces) == 0) & (i > 0)
        left = jnp.maximum(owner - 1, 0)

        @pl.when(margin & (left != me))
        def _():
            act(part_copy(i, 0, 1, left, per_tile, 1))

        if keep:
            @pl.when(margin & (left == me))
            def _():
                parts[me, per_tile] = outb[i * per]

    def over(w, sheared):
        clear = 1.0 - acc[w, flat - rows :, :]
        for c in range(channels):
            acc[w, c * rows : (c + 1) * rows, :] += clear * sheared[c * rows : (c + 1) * rows]

    def store(i, w, at):
        x = i * CHUNK + w * LANES - LEAD + iota((flat, LANES), 1)
        outb[at] = jnp.where((x >= 0) & (x < cols), acc[w], 0.0).astype(BF)

    @pl.loop(0, chunks)
    def _(i):
        @pl.when(has_up)
        def _():
            up_copy(i).wait_recv()
            work[:groups] = recv_up[i]

        @pl.when(has_dn)
        def _():
            dn_copy(i).wait_recv()
            work[groups:] = recv_dn[i]

        acc[...] = jnp.zeros_like(acc)

        @pl.loop(0, slab)
        def _(k):
            _, _, g0, g1 = groups_of(row_s[k], off_up[k], off_dn[k], groups)
            band[k, :, :LANES] = band[k, :, CHUNK:]
            opacity = vol[i, channels - 1, k]
            own = [vol[i, c, k] * opacity for c in range(channels - 1)] + [opacity]
            data = jnp.concatenate(own + [work[g0], work[g1]], 0)
            weights = w_row[k, :, : flat + 2 * channels * GROUP]
            new = jnp.dot(weights, data, preferred_element_type=F32).astype(BF)
            band[k, :, LANES:] = new
            stack = [band[k, :, w * LANES : (w + 2) * LANES] for w in range(per)]
            sheared = jnp.dot(jnp.concatenate(stack, 0), w_col[k], preferred_element_type=F32)
            for w in range(per):
                over(w, sheared[w * flat : (w + 1) * flat])

        for w in range(per):
            store(i, w, i * per + w)

        @pl.when(i > 0)
        def _():
            deliver(i - 1, lambda copy: copy.start(), True)

    deliver(jnp.int32(chunks - 1), lambda copy: copy.start(), True)

    acc[0] = jnp.zeros_like(acc[0])

    @pl.loop(0, slab)
    def _(k):
        sheared = jnp.dot(band[k, :, CHUNK:], w_col[k, :LANES], preferred_element_type=F32)
        over(0, sheared)

    store(chunks, 0, chunks * per)

    def tail_copy():
        return pltpu.make_async_remote_copy(
            outb.at[pl.ds(chunks * per, 1)],
            parts.at[me, pl.ds(per_tile, 1)],
            s_part.at[chunks, 1],
            r_part.at[me, pieces],
            device_id=(jnp.int32(depth - 1), row),
            device_id_type=MESH,
        )

    @pl.when(me != depth - 1)
    def _():
        tail_copy().start()

    @pl.when(me == depth - 1)
    def _():
        parts[me, per_tile] = outb[chunks * per]

    for d in range(depth):
        @pl.when(me != d)
        def _():
            for p in range(pieces + 1):
                count = per if p < pieces else 1
                pltpu.make_async_remote_copy(
                    outb.at[pl.ds(0, count)],
                    parts.at[d, pl.ds(p * per, count)],
                    s_part.at[0, 0],
                    r_part.at[d, p],
                    device_id=(me, row),
                    device_id_type=MESH,
                ).wait_recv()

    for w in range(per_tile + 1):
        image = parts[0, w].astype(F32)
        image = image.reshape(channels, rows, LANES)
        for d in range(1, depth):
            back = parts[d, w].astype(F32).reshape(channels, rows, LANES)
            image = image + (1.0 - image[channels - 1 :]) * back
        wide_ref[:, w * LANES : (w + 1) * LANES] = image.reshape(flat, LANES)

    width = wide_ref.shape[1]
    amount = warp_ref[...] + SHIFT
    for c in range(channels):
        line = wide_ref[c * rows : (c + 1) * rows]
        line = 0.5 * line + 0.25 * (pltpu.roll(line, 1, 1) + pltpu.roll(line, width - 1, 1))
        line = pltpu.roll(line, width - (LEAD - SHIFT), 1)
        for bit in (1, 2, 4, 8, 16):
            line = jnp.where((amount & bit) != 0, pltpu.roll(line, width - bit, 1), line)
        across = line[:, :tile]
        mid_ref[c] = across
        low_ref[c] = across[:EDGE].astype(BF)
        high_ref[c] = across[rows - EDGE :].astype(BF)

    @pl.loop(0, chunks)
    def _(i):
        @pl.when(has_dn)
        def _():
            up_copy(i).wait_send()

        @pl.when(has_up)
        def _():
            dn_copy(i).wait_send()

        deliver(i, lambda copy: copy.wait_send(), False)

    @pl.when(me != depth - 1)
    def _():
        tail_copy().wait_send()


def slab_stage(high, number, depth, n_rows, volume, scalars, at_up, at_dn, warp):
    channels, slab, rows, cols = volume.shape
    chunks = cols // CHUNK
    groups = high // GROUP
    per = CHUNK // LANES
    tile = cols // depth
    flat = channels * rows
    pieces = tile // CHUNK
    smem = pl.BlockSpec(memory_space=pltpu.SMEM)
    vmem = pl.BlockSpec(memory_space=pltpu.VMEM)
    halo = pltpu.VMEM((chunks, groups, channels * GROUP, CHUNK), BF)
    half = jax.ShapeDtypeStruct((channels, EDGE, tile), BF)
    dma = pltpu.SemaphoreType.DMA
    return pl.pallas_call(
        functools.partial(slab_kernel, (depth, n_rows)),
        in_specs=[smem] * 4 + [vmem] * 3 + [pl.BlockSpec(memory_space=pl.ANY)],
        out_specs=[vmem] * 3,
        out_shape=[jax.ShapeDtypeStruct((channels, rows, tile), F32), half, half],
        scratch_shapes=[
            pltpu.VMEM((chunks, channels, slab, rows, CHUNK), BF),
            halo,
            halo,
            halo,
            halo,
            pltpu.VMEM((2 * groups, channels * GROUP, CHUNK), BF),
            pltpu.VMEM((slab, flat, 2 * LANES), BF),
            pltpu.VMEM((slab, 2 * LANES, LANES), BF),
            pltpu.VMEM((slab, flat, LANES + CHUNK), BF),
            pltpu.VMEM((per, flat, LANES), F32),
            pltpu.VMEM((chunks * per + 1, flat, LANES), BF),
            pltpu.VMEM((depth, tile // LANES + 1, flat, LANES), BF),
            pltpu.VMEM((flat, tile + LANES), F32),
            dma((chunks,)),
            dma((chunks,)),
            dma((chunks,)),
            dma((chunks,)),
            dma((chunks,)),
            dma((chunks + 1, 2)),
            dma((depth, pieces + 1)),
        ],
        compiler_params=pltpu.CompilerParams(
            collective_id=number, has_side_effects=True, vmem_limit_bytes=60 * 2**20
        ),
        name=f"slab_{high}",
    )(*scalars, at_up, at_dn, warp, volume)


def final_kernel(shift_ref, mid_ref, low_ref, high_ref, out_ref, ext_ref):
    channels, rows, tile = mid_ref.shape
    shifts = shift_ref[...]
    for c in range(channels):
        ext_ref[:EDGE] = low_ref[c].astype(F32)
        ext_ref[EDGE : EDGE + rows] = mid_ref[c]
        ext_ref[EDGE + rows :] = high_ref[c].astype(F32)
        moved = jnp.zeros((rows + 2, tile), F32)
        for v in range(-SHIFT, SHIFT + 1):
            start = EDGE + v - 1
            moved = jnp.where(shifts == v, ext_ref[start : start + rows + 2], moved)
        out_ref[c] = 0.5 * moved[1 : rows + 1] + 0.25 * (moved[:rows] + moved[2 : rows + 2])


def final_rows(mid, low, high, shifts):
    channels, rows, tile = mid.shape
    block = 256
    return pl.pallas_call(
        final_kernel,
        grid=(tile // block,),
        in_specs=[
            pl.BlockSpec((1, block), lambda i: (0, i)),
            pl.BlockSpec((channels, rows, block), lambda i: (0, 0, i)),
            pl.BlockSpec((channels, EDGE, block), lambda i: (0, 0, i)),
            pl.BlockSpec((channels, EDGE, block), lambda i: (0, 0, i)),
        ],
        out_specs=pl.BlockSpec((channels, rows, block), lambda i: (0, 0, i)),
        out_shape=jax.ShapeDtypeStruct((channels, rows, tile), F32),
        scratch_shapes=[pltpu.VMEM((rows + 2 * EDGE, block), F32)],
        name="final_rows",
    )(shifts, mid, low, high)


def neighbours(axis):
    count = lax.axis_size(axis)
    forward = [(i, i + 1) for i in range(count - 1)]
    return forward, [(b, a) for a, b in forward]


def swapped(value, axis, mask):
    pairs = [(source, source ^ mask) for source in range(lax.axis_size(axis))]
    return lax.ppermute(value, axis, pairs)


def classes_of(slab):
    top = -(-slab * RIM // GROUP) * GROUP
    rough = {int(slab * f) // GROUP * GROUP for f in (3.5, 4, 4.5, 5.5)}
    return sorted({h for h in rough if h >= 2 * GROUP} | {top})


def per_device(volume, shear_rows, shear_cols, warp_cols, warp_rows):
    channels, slab, rows, cols = volume.shape
    depth = lax.axis_size("depth")
    n_rows = lax.axis_size("rows")
    forward, backward = neighbours("rows")

    n_up = jnp.maximum(0, shear_rows + 1)
    n_dn = jnp.maximum(0, 1 - shear_rows)
    end_up = jnp.cumsum(n_up)
    end_dn = jnp.cumsum(n_dn)
    off_up = end_up - n_up
    off_dn = end_dn - n_dn
    need = jnp.maximum(end_up[-1], end_dn[-1]).astype(jnp.int32)
    for other in [swapped(need, "depth", m) for m in range(1, depth)]:
        need = jnp.maximum(need, other)
    row = jnp.arange(EDGE, dtype=jnp.int32)
    at_up = jnp.where(row[None] < n_up[:, None], off_up[:, None] + row[None], -1).reshape(1, -1)
    back = row[None] - (EDGE - n_dn[:, None])
    at_dn = jnp.where(back >= 0, off_dn[:, None] + back, -1).reshape(1, -1)
    row_start = lax.axis_index("rows") * rows
    warp = lax.dynamic_slice_in_dim(warp_cols, row_start, rows, 0).reshape(rows, 1)
    scalars = (shear_rows, shear_cols, off_up, off_dn)

    sizes = classes_of(slab)
    which = sum((need > size).astype(jnp.int32) for size in sizes[:-1])
    branches = [
        functools.partial(slab_stage, size, number + 1, depth, n_rows)
        for number, size in enumerate(sizes)
    ]
    mid, low, high = lax.switch(which, branches, volume, scalars, at_up, at_dn, warp)
    under = lax.ppermute(high, "rows", forward)
    above = lax.ppermute(low, "rows", backward)
    return final_rows(mid, under, above, warp_rows.reshape(1, -1))


def solution(mesh):
    return jax.shard_map(
        per_device,
        mesh=mesh,
        in_specs=(P(None, "depth", "rows", None), P("depth"), P("depth"), P(), P("depth")),
        out_specs=P(None, "rows", "depth"),
        check_vma=False,
    )
```

profile of v0, /device:TPU:19, one launch (start us, length us, event | category | flops | bytes accessed | tf_op | source)
XLA Modules:
  0.0 173.8 jit_solution(4028011352546886142)
XLA Ops:
  0.0 0.0 copy-start
  0.0 0.7 fusion.2
  0.7 0.1 copy.14
  0.8 0.5 slice.11
  1.3 0.1 reduce.1
  1.5 0.7 broadcast_subtract_fusion
  2.1 0.1 copy.13
  2.2 0.5 slice.10
  4.0 1.6 collective-permute-start.2
  5.6 1.9 %collective-permute-start.1 = (s32[]{:T(128)}, s32[]{:T(128)}, u32[]{:S(2)}, u32[]{:S(2)}) collective-permute-start(s32[]{:T(128)} %bitcast.3), channel_id=1, source_target_pairs={{0,16},{8,24},{16,0},{24,8},{1,17},{9,25},{17,1},{25,9},{2,18},{10... | collective-permute-start | bytes 20 | tf_op jit(solution)/shard_map/ppermute | solution.py:396
  7.6 2.1 %collective-permute-start = (s32[]{:T(128)}, s32[]{:T(128)}, u32[]{:S(2)}, u32[]{:S(2)}) collective-permute-start(s32[]{:T(128)} %bitcast.3), channel_id=1, source_target_pairs={{0,8},{8,0},{16,24},{24,16},{1,9},{9,1},{17,25},{25,17},{2,10},{10... | collective-permute-start | bytes 20 | tf_op jit(solution)/shard_map/ppermute | solution.py:396
  9.7 0.1 reduce
  9.8 0.7 fusion.3
  10.4 0.1 add_select_fusion
  10.5 0.1 select_n.33
  10.6 0.1 select_n.31
  10.7 0.0 copy-done
  10.7 0.1 dynamic-slice_bitcast_fusion
  10.8 0.0 collective-permute-done
  11.4 0.0 collective-permute-done.1
  12.0 0.0 collective-permute-done.2
  12.7 147.4 %conditional.1 = ((f32[4,32,1024]{2,1,0:T(8,128)S(1)}, bf16[4,16,1024]{2,1,0:T(8,128)(2,1)S(1)}, bf16[4,16,1024]{2,1,0:T(8,128)(2,1)S(1)})) conditional(s32[]{:T(128)} %clamp.3, (s32[16]{0:T(128)}, s32[16]{0:T(128)}, s32[16]{0:T(128)S(1)}, s32[16]{0:T(128)S(1)}, s32[1,256]{1,0:T(1,128)S(1)}, ...), branch_computations={%region_2.3_spmd, %region_3.4_spmd, %region_4.5_spmd, %region_5.6_... | conditional | bytes 264 | solution.py:434
  12.7 0.7 copy.18.warp_ref
  13.4 146.3 %slab_88.1 = (f32[4,32,1024]{2,1,0:T(8,128)S(1)}, bf16[4,16,1024]{2,1,0:T(8,128)(2,1)S(1)}, bf16[4,16,1024]{2,1,0:T(8,128)(2,1)S(1)}) custom-call(s32[16]{0:T(128)} %get-tuple-element.109.row_s, s32[16]{0:T(128)} %get-tuple-element.110.col_s, s32[16]{0:T(128)S(1)} %get-tuple-element.111.off_up, s32[16]{0:T(128)S(1)} %get-tuple-element.112.off_dn, ...), custom_call_target="tpu_custom_call" | custom-call | tf_op jit(solution)/shard_map/cond/branch_3_fun/slab_88/pallas_call | solution.py:321
  160.1 2.0 %collective-permute-start.3 = (bf16[4,16,1024]{2,1,0:T(8,128)(2,1)S(1)}, bf16[4,16,1024]{2,1,0:T(8,128)(2,1)S(1)}, u32[]{:S(2)}, u32[]{:S(2)}) collective-permute-start(bf16[4,16,1024]{2,1,0:T(8,128)(2,1)S(1)} %get-tuple-element.129), channel_id=1, source_target_pairs={{0,1},{1,2},{2,3},{3,4},{4,5},{5,6},{6,7},{8,9},{9,10},{10,11},{11... | collective-permute-start | bytes 393224 | tf_op jit(solution)/shard_map/ppermute | solution.py:435
  162.1 4.2 %collective-permute-start.4 = (bf16[4,16,1024]{2,1,0:T(8,128)(2,1)S(1)}, bf16[4,16,1024]{2,1,0:T(8,128)(2,1)S(1)}, u32[]{:S(2)}, u32[]{:S(2)}) collective-permute-start(bf16[4,16,1024]{2,1,0:T(8,128)(2,1)S(1)} %get-tuple-element.130), channel_id=1, source_target_pairs={{1,0},{2,1},{3,2},{4,3},{5,4},{6,5},{7,6},{9,8},{10,9},{11,10},{12... | collective-permute-start | bytes 393224 | tf_op jit(solution)/shard_map/ppermute | solution.py:436
  166.3 0.5 collective-permute-done.3.low_ref
  166.8 0.0 copy-start.1
  166.8 2.7 %collective-permute-done.4.high_ref = bf16[4,16,1024]{2,1,0:T(8,128)(2,1)S(1)} collective-permute-done((bf16[4,16,1024]{2,1,0:T(8,128)(2,1)S(1)}, bf16[4,16,1024]{2,1,0:T(8,128)(2,1)S(1)}, u32[]{:S(2)}, u32[]{:S(2)}) %collective-permute-start.4) | collective-permute-done | bytes 131104 | tf_op jit(solution)/shard_map/ppermute | solution.py:436
  169.5 0.0 copy-start.2
  169.5 0.0 copy-done.1
  169.5 0.6 copy-done.2
  170.2 3.6 %final_rows.1 = f32[4,32,1024]{2,1,0:T(8,128)} custom-call(s32[1,1024]{1,0:T(1,128)} %bitcast.8, f32[4,32,1024]{2,1,0:T(8,128)S(1)} %get-tuple-element.128.mid_ref, bf16[4,16,1024]{2,1,0:T(8,128)(2,1)} %copy-done.1, bf16[4,16,1024]{2,1,0:T(8,128)(2,1)} %copy-done.2), custom_call_target="tpu_custom_call" | custom-call | tf_op jit(solution)/shard_map/final_rows/pallas_call | solution.py:372
  (2 shorter events, 0.1 us)
Async XLA Ops:
  0.0 10.7 %copy-start = (s32[256]{0:T(256)S(1)}, s32[256]{0:T(256)}, u32[]{:S(2)}) copy-start(s32[256]{0:T(256)} %param.13) | copy-start | bytes 3076
  4.0 8.0 %collective-permute-start.2 = (s32[]{:T(128)}, s32[]{:T(128)}, u32[]{:S(2)}, u32[]{:S(2)}) collective-permute-start(s32[]{:T(128)} %bitcast.3), channel_id=1, source_target_pairs={{0,24},{8,16},{16,8},{24,0},{1,25},{9,17},{17,9},{25,1},{2,26},{10... | collective-permute-start | bytes 20 | tf_op jit(solution)/shard_map/ppermute | solution.py:396
  5.6 5.7 %collective-permute-start.1 = (s32[]{:T(128)}, s32[]{:T(128)}, u32[]{:S(2)}, u32[]{:S(2)}) collective-permute-start(s32[]{:T(128)} %bitcast.3), channel_id=1, source_target_pairs={{0,16},{8,24},{16,0},{24,8},{1,17},{9,25},{17,1},{25,9},{2,18},{10... | collective-permute-start | bytes 20 | tf_op jit(solution)/shard_map/ppermute | solution.py:396
  7.6 3.2 %collective-permute-start = (s32[]{:T(128)}, s32[]{:T(128)}, u32[]{:S(2)}, u32[]{:S(2)}) collective-permute-start(s32[]{:T(128)} %bitcast.3), channel_id=1, source_target_pairs={{0,8},{8,0},{16,24},{24,16},{1,9},{9,1},{17,25},{25,17},{2,10},{10... | collective-permute-start | bytes 20 | tf_op jit(solution)/shard_map/ppermute | solution.py:396
  160.1 6.7 %collective-permute-start.3 = (bf16[4,16,1024]{2,1,0:T(8,128)(2,1)S(1)}, bf16[4,16,1024]{2,1,0:T(8,128)(2,1)S(1)}, u32[]{:S(2)}, u32[]{:S(2)}) collective-permute-start(bf16[4,16,1024]{2,1,0:T(8,128)(2,1)S(1)} %get-tuple-element.129), channel_id=1, source_target_pairs={{0,1},{1,2},{2,3},{3,4},{4,5},{5,6},{6,7},{8,9},{9,10},{10,11},{11... | collective-permute-start | bytes 393224 | tf_op jit(solution)/shard_map/ppermute | solution.py:435
  162.1 7.4 %collective-permute-start.4 = (bf16[4,16,1024]{2,1,0:T(8,128)(2,1)S(1)}, bf16[4,16,1024]{2,1,0:T(8,128)(2,1)S(1)}, u32[]{:S(2)}, u32[]{:S(2)}) collective-permute-start(bf16[4,16,1024]{2,1,0:T(8,128)(2,1)S(1)} %get-tuple-element.130), channel_id=1, source_target_pairs={{1,0},{2,1},{3,2},{4,3},{5,4},{6,5},{7,6},{9,8},{10,9},{11,10},{12... | collective-permute-start | bytes 393224 | tf_op jit(solution)/shard_map/ppermute | solution.py:436
  166.8 2.7 %copy-start.1 = (bf16[4,16,1024]{2,1,0:T(8,128)(2,1)}, bf16[4,16,1024]{2,1,0:T(8,128)(2,1)S(1)}, u32[]{:S(2)}) copy-start(bf16[4,16,1024]{2,1,0:T(8,128)(2,1)S(1)} %collective-permute-done.3.low_ref) | copy-start | bytes 393220
  169.5 0.6 copy-start.2
where the time goes:
time: 175 us; the launch traced here: 174 us
  Pallas kernels  150 us (86%)
  starting transfers between devices  11.8 us (7%)
  between operations  3.24 us (2%)
  waiting for transfers between devices  3.23 us (2%)
  local copies, waits for them, and re-layouts  2.81 us (2%)
  other arithmetic  2.37 us (1%)
    pallas_call x1, Pallas kernels, slab_stage(): pl.pallas_call(functools.partial(slab_kernel, (depth, n_rows)), in_specs=...  146 us
    ppermute x3, starting transfers between devices, swapped(): return lax.ppermute(value, axis, pairs)  5.62 us
    ppermute x1, starting transfers between devices, per_device(): above = lax.ppermute(low, 'rows', backward)  4.15 us
    pallas_call x1, Pallas kernels, final_rows(): pl.pallas_call(final_kernel, grid=(tile // block,), in_specs=[pl.BlockSpe...  3.58 us
  transfers between devices with their start and end apart: 5, of which 2 were waited for; matrix products, arithmetic and copies ran while one was open for 1% of the time, Pallas kernels for 0%

commit v1 on v0

v1 whole, which is shorter than its diff:
```python
import functools

import jax
import jax.numpy as jnp
from jax import lax
from jax.experimental import pallas as pl
from jax.experimental.pallas import tpu as pltpu
from jax.sharding import PartitionSpec as P

SHIFT = 8
RIM = SHIFT + 1
GROUP = 16
EDGE = 16
LANES = 128
LEAD = 16
CHUNK = 512
BLOCK = 8
SLOT = 10
AHEAD = 4
GHOST_LAG = 2
MERGE_LAG = 4
BF = jnp.bfloat16
F32 = jnp.float32
MESH = pl.DeviceIdType.MESH


def weight_of(offset):
    return jnp.where(offset == 0, 0.5, jnp.where(jnp.abs(offset) == 1, 0.25, 0.0)).astype(F32)


def iota(shape, dim):
    return lax.broadcasted_iota(jnp.int32, shape, dim)


def slab_kernel(
    sizes, row_s, col_s, off_up, off_dn, at_ref, slot_ref, warp_ref, vol_hbm,
    mid_ref, low_ref, high_ref,
    vol, a_send, a_recv, t_send, t_recv, c_send, c_recv, spread, own_w, colour_w, w_col, unpack, collect,
    pick_a, pick_t, band_a, band_c, trans, t_all, ghost, acc, outb, parts, wide_ref,
    load_sem, a_ss, a_rs, t_ss, t_rs, c_ss, c_rs, s_part, r_part,
):
    depth, n_rows = sizes
    chunks, channels, slab, rows, _ = vol.shape
    colours = channels - 1
    high = a_send.shape[2]
    cols = chunks * CHUNK
    tile = cols // depth
    per = CHUNK // LANES
    per_tile = tile // LANES
    pieces = tile // CHUNK
    flat = channels * rows
    tint = colours * rows
    step = BLOCK * rows
    me = lax.axis_index("depth")
    row = lax.axis_index("rows")
    has = (row > 0, row < n_rows - 1)
    got = (row < n_rows - 1, row > 0)
    target = (jnp.maximum(row - 1, 0), jnp.minimum(row + 1, n_rows - 1))

    def load_alpha(i):
        at = pl.ds(pl.multiple_of(i * CHUNK, CHUNK), CHUNK)
        return pltpu.make_async_copy(vol_hbm.at[colours, :, :, at], vol.at[i, colours], load_sem.at[0, i])

    def load_colour(i):
        at = pl.ds(pl.multiple_of(i * CHUNK, CHUNK), CHUNK)
        return pltpu.make_async_copy(
            vol_hbm.at[pl.ds(0, colours), :, :, at], vol.at[i, pl.ds(0, colours)], load_sem.at[1, i]
        )

    order = [chunks - 1] + list(range(chunks - 1))
    for i in order:
        load_alpha(i).start()
    for i in order:
        load_colour(i).start()

    barrier = pltpu.get_barrier_semaphore()
    for r in (lax.rem(row + 1, n_rows), lax.rem(row + n_rows - 1, n_rows)):
        pl.semaphore_signal(barrier, inc=1, device_id=(me, r), device_id_type=MESH)
    for m in range(1, depth):
        pl.semaphore_signal(barrier, inc=1, device_id=(lax.rem(me + m, depth), row), device_id_type=MESH)
    pl.semaphore_wait(barrier, depth + 1)

    def message(kind, way, i):
        source, dest, ss, rs = kind
        return pltpu.make_async_remote_copy(
            source.at[way, i], dest.at[way, i], ss.at[way, i], rs.at[way, i],
            device_id=(me, target[way]), device_id_type=MESH,
        )

    def lead_message(way):
        part = pl.ds(0, LANES)
        return pltpu.make_async_remote_copy(
            a_send.at[way, chunks, :, part], a_recv.at[way, chunks, :, part],
            a_ss.at[way, chunks], a_rs.at[way, chunks],
            device_id=(me, target[way]), device_id_type=MESH,
        )

    kind_a = (a_send, a_recv, a_ss, a_rs)
    kind_t = (t_send, t_recv, t_ss, t_rs)
    kind_c = (c_send, c_recv, c_ss, c_rs)

    def start(kind, i):
        for way in range(2):
            @pl.when(has[way])
            def _():
                message(kind, way, i).start()

    def arrived(kind, i):
        for way in range(2):
            @pl.when(got[way])
            def _():
                message(kind, way, i).wait_recv()

    def sent(kind, i):
        for way in range(2):
            @pl.when(has[way])
            def _():
                message(kind, way, i).wait_send()

    firsts = (0, rows - EDGE)
    for way in range(2):
        slots = at_ref[way : way + 1]
        pick_a[way] = (iota((high, slab * EDGE), 0) == slots).astype(F32).astype(BF)

    def pack(i, way, at):
        first = firsts[way]
        source = vol[i, colours, :, first : first + EDGE, at : CHUNK]
        source = source.reshape(slab * EDGE, CHUNK - at)
        return jnp.dot(pick_a[way], source, preferred_element_type=F32).astype(BF)

    load_alpha(chunks - 1).wait()
    for way in range(2):
        a_send[way, chunks, :, :LANES] = pack(chunks - 1, way, CHUNK - LANES)

    @pl.loop(0, chunks)
    def _(i):
        @pl.when(i < chunks - 1)
        def _():
            load_alpha(i).wait()

        for way in range(2):
            a_send[way, i] = pack(i, way, 0)

        @pl.when(i == 0)
        def _():
            for way in range(2):
                @pl.when(has[way])
                def _():
                    lead_message(way).start()

        @pl.when((i > 0) & (i <= AHEAD))
        def _():
            start(kind_a, i - 1)

    for way in range(2):
        @pl.when(jnp.logical_not(got[way]))
        def _():
            a_recv[way] = jnp.zeros(a_recv.shape[1:], BF)
            t_recv[way] = jnp.zeros(t_recv.shape[1:], BF)
            c_recv[way] = jnp.zeros(c_recv.shape[1:], BF)

    lane = iota((high, slab * rows), 0)
    for way in range(2):
        slots = slot_ref[way : way + 1]
        pick_t[way * high : (way + 1) * high] = (lane == slots).astype(F32).astype(BF)
    shape = (2 * rows, slab * rows)
    m = iota(shape, 0)
    j = iota(shape, 1)
    s = slot_ref[2:3]
    e = (j % rows) % SLOT
    side = jnp.where(s > 0, 0, jnp.where(s < 0, 1, jnp.where(e >= SHIFT // 2 + 1, 0, 1)))
    collect[...] = (((m % rows) + rows * (m // rows)) == ((j % rows) + rows * side)).astype(F32).astype(BF)

    @pl.loop(0, slab)
    def _(k):
        s = row_s[k]
        ou = off_up[k]
        od = off_dn[k]
        n_up = jnp.maximum(0, s + 1)
        n_dn = jnp.maximum(0, 1 - s)
        mine = pl.ds(pl.multiple_of(k * rows, rows), rows)
        y = iota((rows, high), 0)
        slot = iota((rows, high), 1)
        u = slot - ou
        keep = (u >= 0) & (u < n_up)
        spread[mine, :high] = jnp.where(keep, weight_of(rows + u - y - s), 0.0).astype(BF)
        v = slot - od
        keep = (v >= 0) & (v < n_dn)
        spread[mine, high:] = jnp.where(keep, weight_of(v - n_dn - y - s), 0.0).astype(BF)
        e = jnp.where(y < colours * SLOT, y % SLOT, -1 - 2 * rows)
        e = jnp.where(e > SHIFT, -1 - 2 * rows, e)
        hit = (v == e) & (v < n_dn) & (v >= 0)
        unpack[mine, :high] = hit.astype(F32).astype(BF)
        hit = (u == e - SHIFT + s) & (u < n_up) & (u >= 0)
        unpack[mine, high:] = hit.astype(F32).astype(BF)
        y = iota((rows, step), 0)
        j = iota((rows, step), 1)
        own_w[mine] = jnp.where(
            (j // rows) == lax.rem(k, BLOCK), weight_of((j % rows) - y - s), 0.0
        ).astype(BF)
        m = iota((flat, tint), 0)
        j = iota((flat, tint), 1)
        e = (m - tint) % SLOT
        north = jnp.where(s > 0, 1, jnp.where(s < 0, 0, jnp.where(e >= SHIFT // 2 + 1, 1, 0)))
        y = jnp.where(m < tint, m % rows, jnp.where(north > 0, e - RIM, rows + e))
        c = jnp.where(m < tint, m // rows, (m - tint) // SLOT)
        same = c == (j // rows)
        colour_w[k] = jnp.where(same, weight_of((j % rows) - y - s), 0.0).astype(BF)
        shape = (2 * LANES, LANES)
        m = iota(shape, 0)
        n = iota(shape, 1)
        w = weight_of(m - n - (LANES - LEAD) - col_s[k])
        w_col[0, k] = w.astype(BF)
        w_col[1, k] = jnp.where(jnp.where(m < LANES, 0, 1) == jnp.where(n < LEAD, 0, 1), w, 0.0).astype(BF)

    def alpha_rows(i, at, to, width):
        halo = jnp.concatenate([a_recv[way, i, :, :width] for way in range(2)], 0)
        source = i if at == 0 else chunks - 1
        for b in range(slab // BLOCK):
            part = slice(b * step, (b + 1) * step)
            own = vol[source, colours, b * BLOCK : (b + 1) * BLOCK, :, at : at + width]
            own = own.reshape(step, width)
            total = jnp.dot(own_w[part], own, preferred_element_type=F32)
            total = total + jnp.dot(spread[part], halo, preferred_element_type=F32)
            band_a[part, to : to + width] = total.astype(BF)

    def colour_rows(i, k, at, width):
        opacity = vol[i, colours, k, :, at : at + width]
        own = [vol[i, c, k, :, at : at + width] * opacity for c in range(colours)]
        return jnp.dot(colour_w[k], jnp.concatenate(own, 0), preferred_element_type=F32).astype(BF)

    for way in range(2):
        @pl.when(got[way])
        def _():
            lead_message(way).wait_recv()

    alpha_rows(chunks, CHUNK - LANES, CHUNK, LANES)
    load_colour(chunks - 1).wait()

    @pl.loop(0, slab)
    def _(k):
        band_c[k, :, CHUNK:] = colour_rows(chunks - 1, k, CHUNK - LANES, LANES)

    def composite(i):
        arrived(kind_a, i)

        @pl.when(i < chunks - 1)
        def _():
            load_colour(i).wait()

        band_a[:, :LANES] = band_a[:, CHUNK:]
        alpha_rows(i, 0, LANES, CHUNK)
        trans[...] = jnp.ones_like(trans)
        acc[i] = jnp.zeros(acc.shape[1:], F32)
        lead = jnp.where(i == 0, 1, 0)

        @pl.loop(0, slab, unroll=4)
        def _(k):
            mine = pl.ds(pl.multiple_of(k * rows, rows), rows)
            band_c[k, :, :LANES] = band_c[k, :, CHUNK:]
            band_c[k, :, LANES:] = colour_rows(i, k, 0, CHUNK)

            def window(w):
                at = slice(w * LANES, (w + 2) * LANES)
                return [band_a[mine, at], band_c[k, :, at]]

            first = jnp.dot(
                jnp.concatenate(window(0), 0), w_col[lead, k], preferred_element_type=F32
            )
            others = sum([window(w) for w in range(1, per)], [])
            rest = jnp.dot(jnp.concatenate(others, 0), w_col[0, k], preferred_element_type=F32)
            tall = rows + flat
            for w in range(per):
                sheared = first if w == 0 else rest[(w - 1) * tall : w * tall]
                at = slice(w * LANES, (w + 1) * LANES)
                t = trans[:, at]
                for c in range(colours):
                    acc[i, c * rows : (c + 1) * rows, at] += t * sheared[(c + 1) * rows : (c + 2) * rows]
                ghost[i, mine, at] = sheared[flat:].astype(BF)
                t_all[mine, at] = t.astype(BF)
                trans[:, at] = t - t * sheared[:rows]

        acc[i, tint:] = 1.0 - trans[...]
        picked = jnp.dot(pick_t[...], t_all[...], preferred_element_type=F32).astype(BF)
        t_send[0, i] = picked[:high]
        t_send[1, i] = picked[high:]

    def ghosts(i):
        arrived(kind_t, i)
        seen = jnp.concatenate([t_recv[0, i], t_recv[1, i]], 0)
        total = None
        for b in range(slab // BLOCK):
            part = slice(b * step, (b + 1) * step)
            t = jnp.dot(unpack[part], seen, preferred_element_type=F32)
            seen_colour = (t * ghost[i, part].astype(F32)).astype(BF)
            value = jnp.dot(collect[:, part], seen_colour, preferred_element_type=F32)
            total = value if total is None else total + value
        total = total.astype(BF)
        c_send[0, i] = total[:rows]
        c_send[1, i] = total[rows:]

    def merge(i):
        arrived(kind_c, i)
        m = iota((tint, 2 * rows), 0)
        j = iota((tint, 2 * rows), 1)
        e = (j % rows) % SLOT
        y = jnp.where(j < rows, rows - RIM + e, e)
        there = (m // rows == (j % rows) // SLOT) & (m % rows == y) & (e <= SHIFT)
        place = there.astype(F32).astype(BF)
        both = jnp.concatenate([c_recv[0, i], c_recv[1, i]], 0)
        more = jnp.dot(place, both, preferred_element_type=F32)
        image = jnp.concatenate([acc[i, :tint] + more, acc[i, tint:]], 0)
        for w in range(per):
            outb[i * per + w] = image[:, w * LANES : (w + 1) * LANES].astype(BF)

        @pl.when(i == 0)
        def _():
            piece = image[:, :LANES]
            n = iota((flat, LANES), 1)
            outb[chunks * per] = jnp.where(n < LEAD, piece, 0.0).astype(BF)
            outb[0] = jnp.where(n < LEAD, 0.0, piece).astype(BF)

    def part_copy(i, source, count, owner, at, margin):
        return pltpu.make_async_remote_copy(
            outb.at[pl.ds(source, count)],
            parts.at[me, pl.ds(at, count)],
            s_part.at[margin, i],
            r_part.at[me, pieces if margin else lax.rem(i, pieces)],
            device_id=(owner, row),
            device_id_type=MESH,
        )

    def deliver(i, act, keep):
        owner = i // pieces
        at = lax.rem(i, pieces) * per

        @pl.when(owner != me)
        def _():
            act(part_copy(i, i * per, per, owner, at, 0))

        if keep:
            @pl.when(owner == me)
            def _():
                parts[me, pl.ds(at, per)] = outb[pl.ds(i * per, per)]

        margin = lax.rem(i, pieces) == 0
        left = lax.rem(owner + depth - 1, depth)
        source = jnp.where(i == 0, chunks * per, i * per)

        @pl.when(margin & (left != me))
        def _():
            act(part_copy(i, source, 1, left, per_tile, 1))

        if keep:
            @pl.when(margin & (left == me))
            def _():
                parts[me, per_tile] = outb[source]

    @pl.loop(0, chunks + MERGE_LAG)
    def _(i):
        @pl.when(i < chunks)
        def _():
            composite(i)

        @pl.when((i >= GHOST_LAG) & (i < chunks + GHOST_LAG))
        def _():
            ghosts(i - GHOST_LAG)

        @pl.when(i < chunks)
        def _():
            start(kind_t, i)

        @pl.when(i + AHEAD < chunks)
        def _():
            start(kind_a, i + AHEAD)

        @pl.when(i > MERGE_LAG)
        def _():
            deliver(i - MERGE_LAG - 1, lambda copy: copy.start(), True)

        @pl.when(i >= MERGE_LAG)
        def _():
            merge(i - MERGE_LAG)

        @pl.when((i >= GHOST_LAG) & (i < chunks + GHOST_LAG))
        def _():
            start(kind_c, i - GHOST_LAG)

    deliver(jnp.int32(chunks - 1), lambda copy: copy.start(), True)

    for d in range(depth):
        @pl.when(me != d)
        def _():
            for p in range(pieces + 1):
                count = per if p < pieces else 1
                pltpu.make_async_remote_copy(
                    outb.at[pl.ds(0, count)],
                    parts.at[d, pl.ds(p * per, count)],
                    s_part.at[0, 0],
                    r_part.at[d, p],
                    device_id=(me, row),
                    device_id_type=MESH,
                ).wait_recv()

    for w in range(per_tile + 1):
        image = parts[0, w].astype(F32)
        image = image.reshape(channels, rows, LANES)
        for d in range(1, depth):
            back = parts[d, w].astype(F32).reshape(channels, rows, LANES)
            image = image + (1.0 - image[channels - 1 :]) * back
        wide_ref[:, w * LANES : (w + 1) * LANES] = image.reshape(flat, LANES)

    width = wide_ref.shape[1]
    amount = warp_ref[...] + SHIFT
    for c in range(channels):
        line = wide_ref[c * rows : (c + 1) * rows]
        line = 0.5 * line + 0.25 * (pltpu.roll(line, 1, 1) + pltpu.roll(line, width - 1, 1))
        line = pltpu.roll(line, width - (LEAD - SHIFT), 1)
        for bit in (1, 2, 4, 8, 16):
            line = jnp.where((amount & bit) != 0, pltpu.roll(line, width - bit, 1), line)
        across = line[:, :tile]
        mid_ref[c] = across
        low_ref[c] = across[:EDGE].astype(BF)
        high_ref[c] = across[rows - EDGE :].astype(BF)

    for way in range(2):
        @pl.when(has[way])
        def _():
            lead_message(way).wait_send()

    @pl.loop(0, chunks)
    def _(i):
        for kind in (kind_a, kind_t, kind_c):
            sent(kind, i)
        deliver(i, lambda copy: copy.wait_send(), False)


def slab_stage(high, number, depth, n_rows, volume, scalars, at, slots, warp):
    channels, slab, rows, cols = volume.shape
    chunks = cols // CHUNK
    per = CHUNK // LANES
    tile = cols // depth
    flat = channels * rows
    tint = flat - rows
    pieces = tile // CHUNK
    smem = pl.BlockSpec(memory_space=pltpu.SMEM)
    vmem = pl.BlockSpec(memory_space=pltpu.VMEM)
    half = jax.ShapeDtypeStruct((channels, EDGE, tile), BF)
    dma = pltpu.SemaphoreType.DMA
    return pl.pallas_call(
        functools.partial(slab_kernel, (depth, n_rows)),
        in_specs=[smem] * 4 + [vmem] * 3 + [pl.BlockSpec(memory_space=pl.ANY)],
        out_specs=[vmem] * 3,
        out_shape=[jax.ShapeDtypeStruct((channels, rows, tile), F32), half, half],
        scratch_shapes=[
            pltpu.VMEM((chunks, channels, slab, rows, CHUNK), BF),
            pltpu.VMEM((2, chunks + 1, high, CHUNK), BF),
            pltpu.VMEM((2, chunks + 1, high, CHUNK), BF),
            pltpu.VMEM((2, chunks, high, CHUNK), BF),
            pltpu.VMEM((2, chunks, high, CHUNK), BF),
            pltpu.VMEM((2, chunks, rows, CHUNK), BF),
            pltpu.VMEM((2, chunks, rows, CHUNK), BF),
            pltpu.VMEM((slab * rows, 2 * high), BF),
            pltpu.VMEM((slab * rows, BLOCK * rows), BF),
            pltpu.VMEM((slab, flat, tint), BF),
            pltpu.VMEM((2, slab, 2 * LANES, LANES), BF),
            pltpu.VMEM((slab * rows, 2 * high), BF),
            pltpu.VMEM((2 * rows, slab * rows), BF),
            pltpu.VMEM((2, high, slab * EDGE), BF),
            pltpu.VMEM((2 * high, slab * rows), BF),
            pltpu.VMEM((slab * rows, LANES + CHUNK), BF),
            pltpu.VMEM((slab, flat, LANES + CHUNK), BF),
            pltpu.VMEM((rows, CHUNK), F32),
            pltpu.VMEM((slab * rows, CHUNK), BF),
            pltpu.VMEM((chunks, slab * rows, CHUNK), BF),
            pltpu.VMEM((chunks, flat, CHUNK), F32),
            pltpu.VMEM((chunks * per + 1, flat, LANES), BF),
            pltpu.VMEM((depth, tile // LANES + 1, flat, LANES), BF),
            pltpu.VMEM((flat, tile + LANES), F32),
            dma((2, chunks)),
            dma((2, chunks + 1)),
            dma((2, chunks + 1)),
            dma((2, chunks)),
            dma((2, chunks)),
            dma((2, chunks)),
            dma((2, chunks)),
            dma((2, chunks)),
            dma((depth, pieces + 1)),
        ],
        compiler_params=pltpu.CompilerParams(
            collective_id=number, has_side_effects=True, vmem_limit_bytes=60 * 2**20
        ),
        name=f"slab_{high}",
    )(*scalars, at, slots, warp, volume)


def final_kernel(shift_ref, mid_ref, low_ref, high_ref, out_ref, ext_ref):
    channels, rows, tile = mid_ref.shape
    shifts = shift_ref[...]
    for c in range(channels):
        ext_ref[:EDGE] = low_ref[c].astype(F32)
        ext_ref[EDGE : EDGE + rows] = mid_ref[c]
        ext_ref[EDGE + rows :] = high_ref[c].astype(F32)
        moved = jnp.zeros((rows + 2, tile), F32)
        for v in range(-SHIFT, SHIFT + 1):
            start = EDGE + v - 1
            moved = jnp.where(shifts == v, ext_ref[start : start + rows + 2], moved)
        out_ref[c] = 0.5 * moved[1 : rows + 1] + 0.25 * (moved[:rows] + moved[2 : rows + 2])


def final_rows(mid, low, high, shifts):
    channels, rows, tile = mid.shape
    block = 256
    return pl.pallas_call(
        final_kernel,
        grid=(tile // block,),
        in_specs=[
            pl.BlockSpec((1, block), lambda i: (0, i)),
            pl.BlockSpec((channels, rows, block), lambda i: (0, 0, i)),
            pl.BlockSpec((channels, EDGE, block), lambda i: (0, 0, i)),
            pl.BlockSpec((channels, EDGE, block), lambda i: (0, 0, i)),
        ],
        out_specs=pl.BlockSpec((channels, rows, block), lambda i: (0, 0, i)),
        out_shape=jax.ShapeDtypeStruct((channels, rows, tile), F32),
        scratch_shapes=[pltpu.VMEM((rows + 2 * EDGE, block), F32)],
        name="final_rows",
    )(shifts, mid, low, high)


def neighbours(axis):
    count = lax.axis_size(axis)
    forward = [(i, i + 1) for i in range(count - 1)]
    return forward, [(b, a) for a, b in forward]


def swapped(value, axis, mask):
    pairs = [(source, source ^ mask) for source in range(lax.axis_size(axis))]
    return lax.ppermute(value, axis, pairs)


def classes_of(slab):
    top = -(-slab * RIM // GROUP) * GROUP
    rough = {int(slab * f) // GROUP * GROUP for f in (3, 4, 5, 6)}
    return sorted({h for h in rough if h >= 2 * GROUP} | {top})


def per_device(volume, shear_rows, shear_cols, warp_cols, warp_rows):
    channels, slab, rows, cols = volume.shape
    depth = lax.axis_size("depth")
    n_rows = lax.axis_size("rows")
    forward, backward = neighbours("rows")

    n_up = jnp.maximum(0, shear_rows + 1)
    n_dn = jnp.maximum(0, 1 - shear_rows)
    end_up = jnp.cumsum(n_up)
    end_dn = jnp.cumsum(n_dn)
    off_up = end_up - n_up
    off_dn = end_dn - n_dn
    need = jnp.maximum(end_up[-1], end_dn[-1]).astype(jnp.int32)
    for other in [swapped(need, "depth", m) for m in range(1, depth)]:
        need = jnp.maximum(need, other)
    row = jnp.arange(EDGE, dtype=jnp.int32)
    at_up = jnp.where(row[None] < n_up[:, None], off_up[:, None] + row[None], -1)
    back = row[None] - (EDGE - n_dn[:, None])
    at_dn = jnp.where(back >= 0, off_dn[:, None] + back, -1)
    at = jnp.stack([at_up, at_dn]).reshape(2, -1)
    y = jnp.arange(rows, dtype=jnp.int32)[None]
    north = jnp.where(y < n_dn[:, None], off_dn[:, None] + y, -1)
    back = y - (rows - n_up[:, None])
    south = jnp.where(back >= 0, off_up[:, None] + back, -1)
    slots = jnp.stack([north, south, jnp.broadcast_to(shear_rows[:, None], north.shape)]).reshape(3, -1)
    row_start = lax.axis_index("rows") * rows
    warp = lax.dynamic_slice_in_dim(warp_cols, row_start, rows, 0).reshape(rows, 1)
    scalars = (shear_rows, shear_cols, off_up, off_dn)

    sizes = classes_of(slab)
    which = sum((need > size).astype(jnp.int32) for size in sizes[:-1])
    branches = [
        functools.partial(slab_stage, size, number + 1, depth, n_rows)
        for number, size in enumerate(sizes)
    ]
    mid, low, high = lax.switch(which, branches, volume, scalars, at, slots, warp)
    under = lax.ppermute(high, "rows", forward)
    above = lax.ppermute(low, "rows", backward)
    return final_rows(mid, under, above, warp_rows.reshape(1, -1))


def solution(mesh):
    return jax.shard_map(
        per_device,
        mesh=mesh,
        in_specs=(P(None, "depth", "rows", None), P("depth"), P("depth"), P(), P("depth")),
        out_specs=P(None, "rows", "depth"),
        check_vma=False,
    )
```

time: 175 us -> 110 us (0.63)
  Pallas kernels: 150 us -> 82.3 us
  local copies, waits for them, and re-layouts: 2.81 us -> 4.84 us
    pallas_call x1, Pallas kernels: 146 us -> 78.7 us  [slab_stage(): pl.pallas_call(functools.partial(slab_kernel, (depth, n_rows)), in_specs=...]
  transfers between devices with their start and end apart: 5 -> 5, of which waited for: 2 -> 2; matrix products, arithmetic and copies ran while one was open for 1% -> 3% of each run, Pallas kernels for 0% -> 0%
where the time goes in v1:
time: 110 us; the launch traced here: 109 us
  Pallas kernels  82.3 us (75%)
  starting transfers between devices  11.9 us (11%)
  local copies, waits for them, and re-layouts  4.84 us (4%)
  waiting for transfers between devices  4.6 us (4%)
  between operations  3.15 us (3%)
  other arithmetic  1.69 us (2%)
    pallas_call x1, Pallas kernels, slab_stage(): pl.pallas_call(functools.partial(slab_kernel, (depth, n_rows)), in_specs=...  78.7 us
    ppermute x3, starting transfers between devices, swapped(): return lax.ppermute(value, axis, pairs)  5.75 us
    pallas_call x1, Pallas kernels, final_rows(): pl.pallas_call(final_kernel, grid=(tile // block,), in_specs=[pl.BlockSpe...  3.58 us
    ppermute x1, starting transfers between devices, per_device(): above = lax.ppermute(low, 'rows', backward)  3.25 us
    ppermute x1, starting transfers between devices, per_device(): under = lax.ppermute(high, 'rows', forward)  2.93 us
    ppermute x1, waiting for transfers between devices, per_device(): above = lax.ppermute(low, 'rows', backward)  2.93 us
  transfers between devices with their start and end apart: 5, of which 2 were waited for; matrix products, arithmetic and copies ran while one was open for 3% of the time, Pallas kernels for 0%

profile of v1, /device:TPU:19, one launch (start us, length us, event | category | flops | bytes accessed | tf_op | source)
XLA Modules:
  0.0 108.8 jit_solution(5656677738737311100)
XLA Ops:
  0.0 0.0 copy-start
  0.0 0.7 subtract_maximum_fusion
  0.7 0.1 copy.14
  0.8 0.5 slice.11
  1.3 0.1 copy.13
  1.5 0.5 slice.10
  3.2 1.6 %collective-permute-start.2 = (s32[]{:T(128)}, s32[]{:T(128)}, u32[]{:S(2)}, u32[]{:S(2)}) collective-permute-start(s32[]{:T(128)} %bitcast.3), channel_id=1, source_target_pairs={{0,24},{8,16},{16,8},{24,0},{1,25},{9,17},{17,9},{25,1},{2,26},{10... | collective-permute-start | bytes 20 | tf_op jit(solution)/shard_map/ppermute | solution.py:538
  4.8 1.9 %collective-permute-start.1 = (s32[]{:T(128)}, s32[]{:T(128)}, u32[]{:S(2)}, u32[]{:S(2)}) collective-permute-start(s32[]{:T(128)} %bitcast.3), channel_id=1, source_target_pairs={{0,16},{8,24},{16,0},{24,8},{1,17},{9,25},{17,1},{25,9},{2,18},{10... | collective-permute-start | bytes 20 | tf_op jit(solution)/shard_map/ppermute | solution.py:538
  6.8 2.2 %collective-permute-start = (s32[]{:T(128)}, s32[]{:T(128)}, u32[]{:S(2)}, u32[]{:S(2)}) collective-permute-start(s32[]{:T(128)} %bitcast.3), channel_id=1, source_target_pairs={{0,8},{8,0},{16,24},{24,16},{1,9},{9,1},{17,25},{25,17},{2,10},{10... | collective-permute-start | bytes 20 | tf_op jit(solution)/shard_map/ppermute | solution.py:538
  9.0 0.1 reduce.1
  9.1 0.1 reduce
  9.2 0.1 lt.76
  9.3 0.1 lt.77
  9.4 0.1 sub.63
  9.4 0.1 sub.64
  9.5 0.7 fusion.2
  10.2 0.1 add.103
  10.3 0.1 add.104
  10.4 0.1 add.100
  10.4 0.1 add.101
  10.5 0.1 add.106
  10.6 0.1 add.107
  10.7 0.1 add.97
  10.7 0.1 add.98
  10.8 0.1 sub.67
  10.9 0.1 sub.68
  11.0 0.1 lt.71
  11.0 0.1 lt.72
  11.1 0.7 stack_broadcast_in_dim.7
  11.9 0.1 stack_broadcast_in_dim.8
  11.9 0.1 lt.75
  12.0 0.1 lt.70
  12.1 0.0 copy-done
  12.1 0.1 dynamic-slice_bitcast_fusion
  12.2 0.0 collective-permute-done
  12.8 0.0 collective-permute-done.1
  13.4 0.0 collective-permute-done.2
  14.1 79.7 %conditional.1 = ((f32[4,32,1024]{2,1,0:T(8,128)S(1)}, bf16[4,16,1024]{2,1,0:T(8,128)(2,1)S(1)}, bf16[4,16,1024]{2,1,0:T(8,128)(2,1)S(1)})) conditional(s32[]{:T(128)} %clamp.3, (s32[16]{0:T(128)}, s32[16]{0:T(128)}, s32[16]{0:T(128)S(1)}, s32[16]{0:T(128)S(1)}, s32[2,256]{1,0:T(2,128)S(1)}, ...), branch_computations={%region_2.3_spmd, %region_3.4_spmd, %region_4.5_spmd, %region_5.6_... | conditional | bytes 264 | solution.py:582
  14.1 0.7 copy.16.warp_ref
  14.8 78.7 %slab_64.1 = (f32[4,32,1024]{2,1,0:T(8,128)S(1)}, bf16[4,16,1024]{2,1,0:T(8,128)(2,1)S(1)}, bf16[4,16,1024]{2,1,0:T(8,128)(2,1)S(1)}) custom-call(s32[16]{0:T(128)} %get-tuple-element.93.row_s, s32[16]{0:T(128)} %get-tuple-element.94.col_s, s32[16]{0:T(128)S(1)} %get-tuple-element.95.off_up, s32[16]{0:T(128)S(1)} %get-tuple-element.96.off_dn, ...), custom_call_target="tpu_custom_call" | custom-call | tf_op jit(solution)/shard_map/cond/branch_1_fun/slab_64/pallas_call | solution.py:450
  93.8 2.9 %collective-permute-start.3 = (bf16[4,16,1024]{2,1,0:T(8,128)(2,1)S(1)}, bf16[4,16,1024]{2,1,0:T(8,128)(2,1)S(1)}, u32[]{:S(2)}, u32[]{:S(2)}) collective-permute-start(bf16[4,16,1024]{2,1,0:T(8,128)(2,1)S(1)} %get-tuple-element.129), channel_id=1, source_target_pairs={{0,1},{1,2},{2,3},{3,4},{4,5},{5,6},{6,7},{8,9},{9,10},{10,11},{11... | collective-permute-start | bytes 393224 | tf_op jit(solution)/shard_map/ppermute | solution.py:583
  96.7 3.2 %collective-permute-start.4 = (bf16[4,16,1024]{2,1,0:T(8,128)(2,1)S(1)}, bf16[4,16,1024]{2,1,0:T(8,128)(2,1)S(1)}, u32[]{:S(2)}, u32[]{:S(2)}) collective-permute-start(bf16[4,16,1024]{2,1,0:T(8,128)(2,1)S(1)} %get-tuple-element.130), channel_id=1, source_target_pairs={{1,0},{2,1},{3,2},{4,3},{5,4},{6,5},{7,6},{9,8},{10,9},{11,10},{12... | collective-permute-start | bytes 393224 | tf_op jit(solution)/shard_map/ppermute | solution.py:584
  100.0 1.7 %collective-permute-done.3.low_ref = bf16[4,16,1024]{2,1,0:T(8,128)(2,1)S(1)} collective-permute-done((bf16[4,16,1024]{2,1,0:T(8,128)(2,1)S(1)}, bf16[4,16,1024]{2,1,0:T(8,128)(2,1)S(1)}, u32[]{:S(2)}, u32[]{:S(2)}) %collective-permute-start.3) | collective-permute-done | bytes 131104 | tf_op jit(solution)/shard_map/ppermute | solution.py:583
  101.6 0.0 copy-start.1
  101.6 2.9 %collective-permute-done.4.high_ref = bf16[4,16,1024]{2,1,0:T(8,128)(2,1)S(1)} collective-permute-done((bf16[4,16,1024]{2,1,0:T(8,128)(2,1)S(1)}, bf16[4,16,1024]{2,1,0:T(8,128)(2,1)S(1)}, u32[]{:S(2)}, u32[]{:S(2)}) %collective-permute-start.4) | collective-permute-done | bytes 131104 | tf_op jit(solution)/shard_map/ppermute | solution.py:584
  104.6 0.0 copy-start.2
  104.6 0.0 copy-done.1
  104.6 0.6 copy-done.2
  105.2 3.6 %final_rows.1 = f32[4,32,1024]{2,1,0:T(8,128)} custom-call(s32[1,1024]{1,0:T(1,128)} %bitcast.24, f32[4,32,1024]{2,1,0:T(8,128)S(1)} %get-tuple-element.128.mid_ref, bf16[4,16,1024]{2,1,0:T(8,128)(2,1)} %copy-done.1, bf16[4,16,1024]{2,1,0:T(8,128)(2,1)} %copy-done.2), custom_call_target="tpu_custom_call" | custom-call | tf_op jit(solution)/shard_map/final_rows/pallas_call | solution.py:514
  (8 shorter events, 0.1 us)
Async XLA Ops:
  0.0 12.1 %copy-start = (s32[256]{0:T(256)S(1)}, s32[256]{0:T(256)}, u32[]{:S(2)}) copy-start(s32[256]{0:T(256)} %param.13) | copy-start | bytes 3076
  3.2 10.2 %collective-permute-start.2 = (s32[]{:T(128)}, s32[]{:T(128)}, u32[]{:S(2)}, u32[]{:S(2)}) collective-permute-start(s32[]{:T(128)} %bitcast.3), channel_id=1, source_target_pairs={{0,24},{8,16},{16,8},{24,0},{1,25},{9,17},{17,9},{25,1},{2,26},{10... | collective-permute-start | bytes 20 | tf_op jit(solution)/shard_map/ppermute | solution.py:538
  4.8 8.0 %collective-permute-start.1 = (s32[]{:T(128)}, s32[]{:T(128)}, u32[]{:S(2)}, u32[]{:S(2)}) collective-permute-start(s32[]{:T(128)} %bitcast.3), channel_id=1, source_target_pairs={{0,16},{8,24},{16,0},{24,8},{1,17},{9,25},{17,1},{25,9},{2,18},{10... | collective-permute-start | bytes 20 | tf_op jit(solution)/shard_map/ppermute | solution.py:538
  6.8 5.5 %collective-permute-start = (s32[]{:T(128)}, s32[]{:T(128)}, u32[]{:S(2)}, u32[]{:S(2)}) collective-permute-start(s32[]{:T(128)} %bitcast.3), channel_id=1, source_target_pairs={{0,8},{8,0},{16,24},{24,16},{1,9},{9,1},{17,25},{25,17},{2,10},{10... | collective-permute-start | bytes 20 | tf_op jit(solution)/shard_map/ppermute | solution.py:538
  93.8 7.9 %collective-permute-start.3 = (bf16[4,16,1024]{2,1,0:T(8,128)(2,1)S(1)}, bf16[4,16,1024]{2,1,0:T(8,128)(2,1)S(1)}, u32[]{:S(2)}, u32[]{:S(2)}) collective-permute-start(bf16[4,16,1024]{2,1,0:T(8,128)(2,1)S(1)} %get-tuple-element.129), channel_id=1, source_target_pairs={{0,1},{1,2},{2,3},{3,4},{4,5},{5,6},{6,7},{8,9},{9,10},{10,11},{11... | collective-permute-start | bytes 393224 | tf_op jit(solution)/shard_map/ppermute | solution.py:583
  96.7 7.9 %collective-permute-start.4 = (bf16[4,16,1024]{2,1,0:T(8,128)(2,1)S(1)}, bf16[4,16,1024]{2,1,0:T(8,128)(2,1)S(1)}, u32[]{:S(2)}, u32[]{:S(2)}) collective-permute-start(bf16[4,16,1024]{2,1,0:T(8,128)(2,1)S(1)} %get-tuple-element.130), channel_id=1, source_target_pairs={{1,0},{2,1},{3,2},{4,3},{5,4},{6,5},{7,6},{9,8},{10,9},{11,10},{12... | collective-permute-start | bytes 393224 | tf_op jit(solution)/shard_map/ppermute | solution.py:584
  101.6 2.9 %copy-start.1 = (bf16[4,16,1024]{2,1,0:T(8,128)(2,1)}, bf16[4,16,1024]{2,1,0:T(8,128)(2,1)S(1)}, u32[]{:S(2)}) copy-start(bf16[4,16,1024]{2,1,0:T(8,128)(2,1)S(1)} %collective-permute-done.3.low_ref) | copy-start | bytes 393220
  104.6 0.6 copy-start.2
